TPU v7x, 512 devices: a whole 4x4x16 slice. The times are simulated.
512 devices in a mesh: row: 32 (over z, core), col: 16 (over y, x).
Axes of the slice: x: 4, y: 4, z: 16, core: 2. Of those that a mesh axis runs over, the one named last changes fastest.
Arguments:
- features: bfloat16 [16, 4096, 256], P('col', 'row'), may hold values from -6 to 6
- tiles: bfloat16 [32, 16, 56, 128, 128], P('row', 'col'), may hold values from -0.5 to 0.5
- tile_rows: int32 [32, 16, 56], P('row', 'col'), may hold values from 0 to 15, as said below
- tile_cols: int32 [32, 16, 56], P('row', 'col'), may hold values from 0 to 31, as said below
- tile_count: int32 [32, 16], P('row', 'col'), may hold values from 4 to 56, as said below
- weight: bfloat16 [256, 256], replicated, may hold values from -0.375 to 0.375
- bias: float32 [256], replicated, may hold values from -3 to 3
- cotangent: bfloat16 [32, 2048, 256], P('row', 'col'), may hold values from -6 to 6
- label_mask: int32 [32, 2048], P('row', 'col'), may hold values 0 or 1
Outputs:
- hidden: bfloat16 [32, 2048, 256], P('row', 'col')
- grad_weight: float32 [256, 256], replicated
- grad_bias: float32 [256], replicated
- grad_features: bfloat16 [16, 4096, 256], P('col', 'row')
Inputs may be any that keep to these rules, and one draw needn't show every extreme that they name: `tile_rows`: tile row among the 16 tile rows of a block; the (row, column) positions of one block's slots are all distinct. `tile_cols`: tile column among the 32 tile columns of a block. The live slots of a block are its first tile_count slots; some block has all 56 slots live.
All inputs are finite; a program needn't handle non-finite values. No bound on the sum of `label_mask` on one device may be relied on, other than what follows from the above.
Results may differ from a plain program's by a relative error of at most 0.023.
Values may be sent and summed in bfloat16 or wider, within the bound.
A program may use at most 64 MiB of HBM per device.

v0:
```python
import math

import jax
import jax.numpy as jnp
from jax import lax
from jax.sharding import PartitionSpec as P


def tile_products(block_tiles, take_index, put_index, live_count, source, out_tiles, transpose):
    total_slots = block_tiles.shape[0]
    group = math.gcd(total_slots, 16)
    tile_size = block_tiles.shape[1]
    width = source.shape[-1]
    form = "sij,sif->sjf" if transpose else "sij,sjf->sif"

    def step(turn, accum):
        start = turn * group
        block = lax.dynamic_slice_in_dim(block_tiles, start, group, 0)
        take = lax.dynamic_slice_in_dim(take_index, start, group, 0)
        put = lax.dynamic_slice_in_dim(put_index, start, group, 0)
        live = start + jnp.arange(group, dtype=jnp.int32) < live_count
        picked = jnp.take(source, take, axis=0)
        product = jnp.einsum(form, block, picked, preferred_element_type=jnp.float32)
        product = jnp.where(live[:, None, None], product, 0.0)
        return accum.at[put].add(product)

    turns = (live_count + group - 1) // group
    start_value = jnp.zeros((out_tiles, tile_size, width), jnp.float32)
    return lax.fori_loop(0, turns, step, start_value)


def times_weight_t(values, weight):
    return lax.dot_general(
        values, weight, (((1,), (1,)), ((), ())), preferred_element_type=jnp.float32
    ).astype(jnp.bfloat16)


def on_device(
    features, tiles, tile_rows, tile_cols, tile_count, weight, bias, cotangent, label_mask
):
    tile_size = tiles.shape[-1]
    rows_dev = features.shape[1]
    width = features.shape[2]
    n_row = lax.axis_size("row")
    n_col = lax.axis_size("col")
    own_tiles = tiles[0, 0]
    rows_index = tile_rows[0, 0]
    cols_index = tile_cols[0, 0]
    live_count = tile_count[0, 0]
    gathered = lax.all_gather(features, "row", axis=1, tiled=True)
    source = gathered.reshape(n_row * rows_dev // tile_size, tile_size, width)
    partial_value = tile_products(
        own_tiles, cols_index, rows_index, live_count, source, n_col * rows_dev // tile_size, False
    )
    partial_value = partial_value.reshape(n_col * rows_dev, width)
    summed = lax.psum_scatter(
        partial_value.astype(jnp.bfloat16), "col", scatter_dimension=0, tiled=True
    )
    pre_act = jnp.dot(summed, weight, preferred_element_type=jnp.float32) + bias
    sigma = jax.nn.sigmoid(pre_act)
    hidden = (pre_act * sigma).astype(jnp.bfloat16)
    kept = label_mask[0].astype(jnp.float32)[:, None]
    slope = sigma * (1.0 + pre_act * (1.0 - sigma))
    grad_pre = (cotangent[0].astype(jnp.float32) * kept * slope).astype(jnp.bfloat16)
    local_weight = lax.dot_general(
        summed, grad_pre, (((0,), (0,)), ((), ())), preferred_element_type=jnp.float32
    )
    local_bias = jnp.sum(grad_pre.astype(jnp.float32), axis=0)
    grad_weight, grad_bias = lax.psum((local_weight, local_bias), ("row", "col"))
    scale = 1.0 / math.sqrt(n_row * n_col * rows_dev)
    grad_agg = times_weight_t(grad_pre, weight)
    grad_rows = lax.all_gather(grad_agg[None], "col", axis=1, tiled=True)[0]
    back_source = grad_rows.reshape(n_col * rows_dev // tile_size, tile_size, width)
    back = tile_products(
        own_tiles,
        rows_index,
        cols_index,
        live_count,
        back_source,
        n_row * rows_dev // tile_size,
        True,
    )
    back = back.reshape(n_row * rows_dev, width)
    back = lax.optimization_barrier(back.astype(jnp.bfloat16)).astype(jnp.float32)
    grad_sum = lax.psum_scatter(back.astype(jnp.bfloat16), "row", scatter_dimension=0, tiled=True)
    return (hidden[None], grad_weight * scale, grad_bias * scale, grad_sum[None])


def solution(mesh):
    return jax.shard_map(
        on_device,
        mesh=mesh,
        in_specs=(
            P("col", "row", None),
            P("row", "col", None, None, None),
            P("row", "col", None),
            P("row", "col", None),
            P("row", "col"),
            P(),
            P(),
            P("row", "col", None),
            P("row", "col"),
        ),
        out_specs=(P("row", "col", None), P(), P(), P("col", "row", None)),
        check_vma=False,
    )
```

profile of v0, /device:TPU:1, one launch (start us, length us, event | category | flops | bytes accessed | tf_op | source)
XLA Modules:
  0.0 866.5 jit_solution(1376284081427758743)
XLA Ops:
  7.2 0.0 copy-start
  7.2 0.0 copy-start.4
  7.2 0.0 copy-start.5
  7.2 0.0 copy-start.2
  7.2 0.0 all-gather.4.cloned.1.call-start
  7.3 0.7 all-gather.4.cloned.1.call-update
  7.9 0.0 reduce-scatter.3.cloned.1.call-start
  8.7 78.6 %all-gather.4.cloned.1.call-done = bf16[1,4096,256]{2,1,0:T(8,128)(2,1)} async-done(((bf16[1,128,256]{2,1,0:T(8,128)(2,1)}), bf16[1,4096,256]{2,1,0:T(8,128)(2,1)}) %all-gather.4.cloned.1.call-update) | async-done | bytes 2097168 | tf_op jit(solution)/shard_map/all_gather | solution.py:50
  87.3 1.5 broadcast_in_dim.69
  88.8 0.0 copy-done.2
  88.8 20.0 %while.20 = (s32[]{:T(128)}, f32[16,128,256]{2,1,0:T(8,128)}, s32[]{:T(128)}, s32[56]{0:T(128)S(1)}, s32[]{:T(128)}, /*index=5*/bf16[56,128,128]{2,1,0:T(8,128)(...) while((s32[]{:T(128)}, f32[16,128,256]{2,1,0:T(8,128)}, ...), condition=%wide.region_2.3_spmd, body=%wide.region_0.2_spmd.sunk | while | flops 67896416 | bytes 6034855 | solution.py:29
  88.8 0.7 compare_and_fusion.4
  89.6 2.2 gather_fusion
  91.8 0.4 convolution_select_fusion.4
  92.1 0.1 compare_select_fusion.8
  92.2 3.3 scatter_fusion
  95.5 0.7 compare_and_fusion.4
  96.2 2.2 gather_fusion
  98.4 0.4 convolution_select_fusion.4
  98.8 0.1 compare_select_fusion.8
  98.9 3.3 scatter_fusion
  102.2 0.7 compare_and_fusion.4
  102.9 2.2 gather_fusion
  105.1 0.4 convolution_select_fusion.4
  105.5 0.1 compare_select_fusion.8
  105.5 3.3 scatter_fusion
  108.8 2.7 convert_element_type.42
  111.6 0.0 reduce-scatter.3.cloned.1.call-update
  111.6 0.0 all-gather.6.cloned.1.call-start
  111.6 0.0 copy-done.8
  111.7 106.5 %reduce-scatter.3.cloned.1.call-done = bf16[128,256]{1,0:T(8,128)(2,1)} async-done(((bf16[2048,256]{1,0:T(8,128)(2,1)}), bf16[128,256]{1,0:T(8,128)(2,1)}) %reduce-scatter.3.cloned.1.call-update) | async-done | bytes 65552 | tf_op jit(solution)/shard_map/reduce_scatter | solution.py:56
  218.1 1.7 convert_reduce_fusion
  219.8 0.8 convolution_convert_fusion
  220.7 0.0 all-gather.6.cloned.1.call-update
  220.7 0.0 all-reduce.2.cloned.1.call-start
  220.7 2.9 copy.13
  223.7 0.9 fusion.16
  224.6 0.0 all-reduce.2.cloned.1.call-update
  224.6 0.0 reduce-scatter.5.cloned.1.call-start
  224.6 54.3 %all-gather.6.cloned.1.call-done = bf16[2048,256]{1,0:T(8,128)(2,1)} async-done(((bf16[128,256]{1,0:T(8,128)(2,1)}), bf16[2048,256]{1,0:T(8,128)(2,1)}) %all-gather.6.cloned.1.call-update) | async-done | bytes 1048592 | tf_op jit(solution)/shard_map/all_gather | solution.py:72
  278.9 2.4 broadcast_in_dim.71
  281.3 18.1 %while.21 = (s32[]{:T(128)}, f32[32,128,256]{2,1,0:T(8,128)}, s32[]{:T(128)}, s32[56]{0:T(128)S(1)}, s32[]{:T(128)}, /*index=5*/bf16[56,128,128]{1,2,0:T(8,128)(...) while((s32[]{:T(128)}, f32[32,128,256]{2,1,0:T(8,128)}, ...), condition=%wide.region_9.10_spmd, body=%wide.region_7.9_spmd.sunk | while | flops 67896416 | bytes 6033847 | solution.py:29
  281.3 0.7 compare_and_fusion.5
  282.1 0.6 gather_fusion.1
  282.7 1.3 convolution_select_fusion.5
  284.0 0.1 compare_select_fusion.9
  284.1 3.3 scatter_fusion.1
  287.4 0.7 compare_and_fusion.5
  288.1 0.6 gather_fusion.1
  288.7 1.3 convolution_select_fusion.5
  290.0 0.1 compare_select_fusion.9
  290.1 3.3 scatter_fusion.1
  293.4 0.7 compare_and_fusion.5
  294.1 0.6 gather_fusion.1
  294.7 1.3 convolution_select_fusion.5
  296.0 0.1 compare_select_fusion.9
  296.1 3.3 scatter_fusion.1
  299.4 3.8 convert_element_type.52
  303.2 0.0 reduce-scatter.5.cloned.1.call-update
  303.3 125.4 %psum.15 = f32[256]{0:T(256)S(1)} all-reduce(f32[256]{0:T(256)S(1)} %get-tuple-element.136), channel_id=1, replica_groups=mesh['row'=32,'col'=16] {'row','col'}, use_global_device_ids=true, to_apply=%region_6.7 | all-reduce | flops 256 | bytes 2048 | tf_op jit(solution)/shard_map/psum | solution.py:69
  428.7 0.6 broadcast_multiply_fusion.1
  429.2 321.6 %all-reduce.2.cloned.1.call-done = f32[256,256]{1,0:T(8,128)} async-done(((f32[256,256]{1,0:T(8,128)}), f32[256,256]{1,0:T(8,128)}) %all-reduce.2.cloned.1.call-update) | async-done | bytes 262160 | tf_op jit(solution)/shard_map/psum | solution.py:69
  750.9 1.7 broadcast_multiply_fusion
  752.5 107.4 %reduce-scatter.5.cloned.1.call-done = bf16[128,256]{1,0:T(8,128)(2,1)} async-done(((bf16[4096,256]{1,0:T(8,128)(2,1)}), bf16[128,256]{1,0:T(8,128)(2,1)}) %reduce-scatter.5.cloned.1.call-update) | async-done | bytes 65552 | tf_op jit(solution)/shard_map/reduce_scatter | solution.py:85
  (19 shorter events, 0.1 us)
Async XLA Ops:
  7.2 211.0 %copy-start = (bf16[256,256]{1,0:T(8,128)(2,1)S(1)}, bf16[256,256]{1,0:T(8,128)(2,1)}, u32[]{:S(2)}) copy-start(bf16[256,256]{1,0:T(8,128)(2,1)} %param.18) | copy-start | bytes 393220
  7.2 81.6 %copy-start.4 = (s32[1,1,56]{2,1,0:T(1,128)S(1)}, s32[1,1,56]{2,1,0:T(1,128)}, u32[]{:S(2)}) copy-start(s32[1,1,56]{2,1,0:T(1,128)} %param.15) | copy-start | bytes 676
  7.2 81.6 %copy-start.5 = (s32[1,1,56]{2,1,0:T(1,128)S(1)}, s32[1,1,56]{2,1,0:T(1,128)}, u32[]{:S(2)}) copy-start(s32[1,1,56]{2,1,0:T(1,128)} %param.16) | copy-start | bytes 676
  7.2 81.6 %copy-start.2 = (bf16[1,1,56,128,128]{4,3,2,1,0:T(8,128)(2,1)S(1)}, bf16[1,1,56,128,128]{4,3,2,1,0:T(8,128)(2,1)}, u32[]{:S(2)}) copy-start(bf16[1,1,56,128,128]{4,3,2,1,0:T(8,128)(2,1)} %param.14) | copy-start | bytes 5505028
  7.2 80.1 %all-gather.4.cloned.1.call-start = ((), (), s32[]{:S(2)}) async-start(), calls=%async_computation.2 | async-start | bytes 2162688 | tf_op jit(solution)/shard_map/all_gather | solution.py:50
  7.9 210.2 %reduce-scatter.3.cloned.1.call-start = ((), (), s32[]{:S(2)}) async-start(), calls=%async_computation.3 | async-start | bytes 1114112 | tf_op jit(solution)/shard_map/reduce_scatter | solution.py:56
  108.8 2.8 copy-start.8
  108.8 109.3 %copy-start.6 = (bf16[1,128,256]{2,1,0:T(8,128)(2,1)S(1)}, bf16[1,128,256]{2,1,0:T(8,128)(2,1)}, u32[]{:S(2)}) copy-start(bf16[1,128,256]{2,1,0:T(8,128)(2,1)} %param.20) | copy-start | bytes 196612
  108.8 109.3 %copy-start.7 = (f32[256]{0:T(256)S(1)}, f32[256]{0:T(256)}, u32[]{:S(2)}) copy-start(f32[256]{0:T(256)} %param.19) | copy-start | bytes 3076
  111.6 167.3 %all-gather.6.cloned.1.call-start = ((), (), s32[]{:S(2)}) async-start(), calls=%async_computation.6 | async-start | bytes 1114112 | tf_op jit(solution)/shard_map/all_gather | solution.py:72
  219.8 3.8 copy-start.3
  220.7 530.2 %all-reduce.2.cloned.1.call-start = ((), (), s32[]{:S(2)}) async-start(), calls=%async_computation.4 | async-start | bytes 524288 | tf_op jit(solution)/shard_map/psum | solution.py:69
  224.6 635.3 %reduce-scatter.5.cloned.1.call-start = ((), (), s32[]{:S(2)}) async-start(), calls=%async_computation.5 | async-start | bytes 2162688 | tf_op jit(solution)/shard_map/reduce_scatter | solution.py:85
  278.9 2.4 copy-start.1
Sparse Core Ops, SparseCore 0:
  10.1 77.1 all-gather.3
  111.7 106.3 reduce-scatter.2
  221.7 57.1 all-gather.5
  284.8 466.0 all-reduce.1
  754.1 105.7 reduce-scatter.4
where the time goes:
time: 870 us; the launch traced here: 866 us
  waiting for transfers between devices  669 us (77%)
  blocking collectives  125 us (14%)
  other arithmetic  33.4 us (4%)
  local copies, waits for them, and re-layouts  15.2 us (2%)
  between operations  14.5 us (2%)
    psum x1, waiting for transfers between devices, on_device(): lax.psum((local_weight, local_bias), ('row', 'col'))  322 us
    psum x1, blocking collectives, on_device(): lax.psum((local_weight, local_bias), ('row', 'col'))  125 us
    reduce_scatter x1, waiting for transfers between devices, on_device(): lax.psum_scatter(back.astype(jnp.bfloat16), 'row', scatter_dimension=0, t...  107 us
    reduce_scatter x1, waiting for transfers between devices, on_device(): lax.psum_scatter(partial_value.astype(jnp.bfloat16), 'col', scatter_dimen...  106 us
    all_gather x1, waiting for transfers between devices, on_device(): gathered = lax.all_gather(features, 'row', axis=1, tiled=True)  78.6 us
    all_gather x1, waiting for transfers between devices, on_device(): grad_rows = lax.all_gather(grad_agg[None], 'col', axis=1, tiled=True)[0]  54.3 us
    scatter-add x6, other arithmetic, step(): return accum.at[put].add(product)  19.8 us
  transfers between devices with their start and end apart: 5, of which 5 were waited for; matrix products, arithmetic and copies ran while one was open for 4% of the time, Pallas kernels for 0%

commit v1 on v0

v1 whole, which is shorter than its diff:
```python
import functools
import math

import jax
import jax.numpy as jnp
from jax import lax
from jax.experimental import pallas as pl
from jax.experimental.pallas import tpu as pltpu
from jax.sharding import PartitionSpec as P

MESH = pl.DeviceIdType.MESH
PARTS = 4
F32 = jnp.float32
BF16 = jnp.bfloat16


def order_rows(key, limit):
    size = key.shape[1]
    by_lane = jnp.broadcast_to(key, (size, size))
    by_sub = by_lane.T
    lane = lax.broadcasted_iota(jnp.int32, (size, size), 1)
    sub = lax.broadcasted_iota(jnp.int32, (size, size), 0)
    same_before = jnp.where(by_sub == by_lane, jnp.where(sub < lane, 1, 0), 0)
    before = jnp.where(by_sub < by_lane, 1, same_before)
    rank = jnp.sum(before, axis=0, keepdims=True)
    repeats = jnp.sum(same_before, axis=0, keepdims=True)
    rank_sub = jnp.broadcast_to(rank, (size, size)).T
    repeats_sub = jnp.broadcast_to(repeats, (size, size)).T
    here = rank_sub == lane
    slot = jnp.sum(jnp.where(here, sub, 0), axis=0, keepdims=True)
    first = jnp.sum(jnp.where(here, jnp.where(repeats_sub == 0, 1, 0), 0), axis=0, keepdims=True)
    last = jnp.sum(jnp.where(by_sub <= lane, 1, 0), axis=0, keepdims=True) - 1
    last = jnp.maximum(last, 0)
    present = jnp.sum(jnp.where(by_sub == lane, 1, 0), axis=0, keepdims=True)
    return [slot, first, last, present]


def kernel(
    dims,
    feat_ref, tiles_hbm, rows_s, cols_s, count_s, rows_v, cols_v, weight_ref, bias_ref, cot_ref, mask_ref,
    hidden_ref, gw_ref, gb_ref, gf_ref,
    tiles, tiles_t, source, prod, part, plane, grads, back, mate, stage, landed,
    table_v, table_s, wide, r0, h0, r1, q1, r2, q2, r3, q3, r4, full,
    tile_sem, table_sem,
    z_send, z_recv, c_send, c_recv, x_send, x_recv, g_send, g_recv, m_send, m_recv,
    a_send, a_recv, b_send, b_recv, d_send, d_recv, s_send, s_recv, e_send, e_recv,
):
    nz, n_col, slots, tb, width, group, scale = dims
    half = nz // 2
    piece = tb // PARTS
    row = lax.axis_index("row")
    col = lax.axis_index("col")
    z = row // 2
    core = row - 2 * z
    other = 1 - core
    far = nz // group
    z_up = lax.rem(z + 1, nz)
    z_down = lax.rem(z + nz - 1, nz)
    in_group = lax.rem(z, group)
    which_group = z // group

    def at_z(zz):
        return (2 * zz + core, col)

    mate_id = (2 * z + other, col)

    def peer(j):
        return lax.rem(col + j, n_col)

    def near_z(j):
        return which_group * group + lax.rem(in_group + j, group)

    def far_z(j):
        return lax.rem(which_group + j, far) * group + in_group

    load_tiles = pltpu.make_async_copy(tiles_hbm, tiles, tile_sem)
    load_tiles.start()

    barrier = pltpu.get_barrier_semaphore()

    def greet(who):
        pl.semaphore_signal(barrier, inc=1, device_id=who, device_id_type=MESH)

    greet(at_z(z_up))
    greet(at_z(z_down))
    greet(mate_id)

    @pl.loop(1, n_col)
    def _(j):
        greet((row, peer(j)))

    for j in range(1, group):
        greet(at_z(near_z(j)))
    for j in range(1, far):
        greet(at_z(far_z(j)))
    pl.semaphore_wait(barrier, 3 + (n_col - 1) + (group - 1) + (far - 1))

    def send(src, dst, send_sem, recv_sem, who):
        return pltpu.make_async_remote_copy(
            src_ref=src, dst_ref=dst, send_sem=send_sem, recv_sem=recv_sem, device_id=who, device_id_type=MESH
        )

    def rows_of(q):
        return pl.ds(q * piece, piece)

    def ring_copy(way, step, q):
        step_z = lax.rem(z + nz - step, nz) if way == 0 else lax.rem(z + step, nz)
        block = source.at[2 * step_z + core, rows_of(q)]
        who = at_z(z_up if way == 0 else z_down)
        return send(block, block, z_send.at[way, step, q], z_recv.at[way, step, q], who)

    def mate_copy(which, q):
        block = source.at[2 * which + core, rows_of(q)]
        return send(block, block, c_send.at[which, q], c_recv.at[which, q], mate_id)

    def takes(way, step, q, last):
        return step != last or (q < PARTS // 2) == (way == 0)

    source[row] = feat_ref[...]
    for q in range(PARTS):
        ring_copy(0, 0, q).start()
        ring_copy(1, 0, q).start()
    for q in range(PARTS):
        mate_copy(z, q).start()

    table_v[...] = jnp.zeros_like(table_v)
    table_v[0:1, 0:slots] = rows_v[...]
    table_v[1:2, 0:slots] = cols_v[...]
    live = lax.broadcasted_iota(jnp.int32, (1, tb), 1) < count_s[0, 0]
    row_key = jnp.where(live, table_v[0:1, :], tb)
    col_key = jnp.where(live, table_v[1:2, :], tb)
    lines = order_rows(row_key, tb) + order_rows(col_key, tb)
    for i, line in enumerate(lines):
        table_v[i : i + 1, :] = line
    save_table = pltpu.make_async_copy(table_v, table_s, table_sem)
    save_table.start()

    def ring_step(step, last):
        for q in range(PARTS):
            for way in (0, 1):
                if takes(way, last, q, 1):
                    ring_copy(way, step - 1, q).wait_recv()
                    came = lax.rem(z + nz - step, nz) if way == 0 else lax.rem(z + step, nz)
                    mate_copy(came, q).start()
                if last == 0:
                    ring_copy(way, step, q).start()

    @pl.loop(1, half - 1)
    def _(step):
        ring_step(step, 0)

    step = half - 1
    for q in range(PARTS):
        for way in (0, 1):
            ring_copy(way, step - 1, q).wait_recv()
            came = lax.rem(z + nz - step, nz) if way == 0 else lax.rem(z + step, nz)
            mate_copy(came, q).start()
            if takes(way, step, q, half - 1):
                ring_copy(way, step, q).start()

    load_tiles.wait()

    @pl.loop(0, slots)
    def _(s):
        tiles_t[s] = tiles[s].T

    save_table.wait()

    for q in range(PARTS):
        way = 0 if q < PARTS // 2 else 1
        ring_copy(way, half - 1, q).wait_recv()
        mate_copy(lax.rem(z + half, nz), q).start()

    @pl.loop(0, nz)
    def _(zz):
        for q in range(PARTS):
            block = source.at[2 * zz + other, rows_of(q)]
            send(block, block, c_send.at[zz, q], c_recv.at[zz, q], mate_id).wait_recv()

    def products(blocks, line, index_s, values):
        def one(k, total):
            slot = table_s[line, k]
            product = jnp.dot(blocks[slot], values[index_s[0, slot]], preferred_element_type=F32)
            total = jnp.where(table_s[line + 1, k] == 1, product, total + product)
            prod[k] = total
            return total

        lax.fori_loop(0, slots, one, jnp.zeros((tb, width), F32))

    def run_total(line, i):
        kept = table_s[line + 3, i] > 0
        return jnp.where(kept, prod[table_s[line + 2, i]], 0.0)

    products(tiles, 0, cols_s, source)

    def plane_copy(j):
        return send(part.at[peer(j)], plane.at[col], x_send.at[j], x_recv.at[j], (row, peer(j)))

    def plane_landed(j):
        back_col = lax.rem(col + n_col - j, n_col)
        return send(part.at[peer(j)], plane.at[back_col], x_send.at[j], x_recv.at[j], (row, peer(j)))

    @pl.loop(1, n_col)
    def _(j):
        part[peer(j)] = run_total(0, peer(j)).astype(BF16)
        plane_copy(j).start()

    def add_plane(j, total):
        plane_landed(j).wait_recv()
        return total + plane[lax.rem(col + n_col - j, n_col)].astype(F32)

    summed = lax.fori_loop(1, n_col, add_plane, run_total(0, col)).astype(BF16)

    pre_act = jnp.dot(summed, weight_ref[...], preferred_element_type=F32) + bias_ref[...]
    sigma = jax.nn.sigmoid(pre_act)
    hidden_ref[...] = (pre_act * sigma).astype(BF16)
    kept = jnp.broadcast_to(mask_ref[...].astype(F32), (tb, tb)).T
    kept = jnp.concatenate([kept] * (width // tb), axis=1)
    slope = sigma * (1.0 + pre_act * (1.0 - sigma))
    grad_pre = (cot_ref[...].astype(F32) * kept * slope).astype(BF16)
    grads[col] = lax.dot_general(
        grad_pre, weight_ref[...], (((1,), (1,)), ((), ())), preferred_element_type=F32
    ).astype(BF16)

    def grad_copy(j, source_col):
        block = grads.at[source_col]
        return send(block, block, g_send.at[j], g_recv.at[j], (row, peer(j)))

    @pl.loop(1, n_col)
    def _(j):
        grad_copy(j, col).start()

    wide[:, 0:width] = lax.dot_general(summed, grad_pre, (((0,), (0,)), ((), ())), preferred_element_type=F32)
    wide[:, width:] = lax.dot_general(
        grad_pre, jnp.ones((tb, tb), BF16), (((0,), (0,)), ((), ())), preferred_element_type=F32
    )
    share = width // 2
    slab = share // n_col
    split = send(wide.at[pl.ds(other * share, share)], r0, d_send.at[0], d_recv.at[0], mate_id)
    split.start()
    split.wait_recv()
    h0[...] = wide[pl.ds(pl.multiple_of(core * share, share), share), :] + r0[...]

    def slab_copy(j, source_col):
        rows = pl.ds(peer(j) * slab, slab)
        return send(h0.at[rows], r1.at[source_col], a_send.at[j], a_recv.at[j], (row, peer(j)))

    @pl.loop(1, n_col)
    def _(j):
        slab_copy(j, col).start()

    @pl.loop(1, n_col)
    def _(j):
        grad_copy(j, lax.rem(col + n_col - j, n_col)).wait_recv()

    def add_slab(j, total):
        back_col = lax.rem(col + n_col - j, n_col)
        slab_copy(j, back_col).wait_recv()
        return total + r1[back_col]

    own_slab = h0[pl.ds(pl.multiple_of(col * slab, slab), slab), :]
    q1[...] = lax.fori_loop(1, n_col, add_slab, own_slab)

    def near_copy(j, slot):
        return send(q1, r2.at[slot], b_send.at[j], b_recv.at[j], at_z(near_z(j)))

    def far_copy(j, slot):
        return send(q2, r3.at[slot], b_send.at[group + j], b_recv.at[group + j], at_z(far_z(j)))

    for j in range(1, group):
        near_copy(j, j).start()

    products(tiles_t, 4, rows_s, grads)

    def share_copy(zz, send_to_mate):
        src = back.at[2 * zz + (other if send_to_mate else core)]
        return send(src, mate.at[zz], m_send.at[zz], m_recv.at[zz], mate_id)

    def fill(zz):
        for which in (core, other):
            back[2 * zz + which] = run_total(4, 2 * zz + which).astype(BF16)
        share_copy(zz, True).start()

    fill(lax.rem(z + half, nz))

    @pl.loop(1, half)
    def _(step):
        fill(lax.rem(z + half - step, nz))
        fill(lax.rem(z + half + step, nz))

    fill(z)

    total = q1[...]
    for j in range(1, group):
        near_copy(j, j).wait_recv()
        total = total + r2[j]
    q2[...] = total
    for j in range(1, far):
        far_copy(j, j).start()

    def dest(way, step):
        return lax.rem(z + half - step, nz) if way == 0 else lax.rem(z + half + step, nz)

    def sum_copy(way, step, q):
        rows = rows_of(q)
        who = at_z(z_up if way == 0 else z_down)
        return send(
            stage.at[way, step, rows], landed.at[way, step, rows], s_send.at[way, step, q], s_recv.at[way, step, q], who
        )

    def mine(zz, q):
        rows = rows_of(q)
        return back[2 * zz + core, rows, :].astype(F32) + mate[zz, rows, :].astype(F32)

    def sum_step(way, step, q, has_more):
        rows = rows_of(q)
        total = mine(dest(way, step), q)
        if has_more:
            sum_copy(way, step - 1, q).wait_recv()
            total = total + landed[way, step - 1, rows, :].astype(F32)
        stage[way, step, rows, :] = total.astype(BF16)
        sum_copy(way, step, q).start()

    share_copy(dest(0, 0), False).wait_recv()
    for q in range(PARTS):
        sum_step(0 if q < PARTS // 2 else 1, 0, q, False)
    share_copy(dest(0, 1), False).wait_recv()
    share_copy(dest(1, 1), False).wait_recv()
    for q in range(PARTS):
        for way in (0, 1):
            sum_step(way, 1, q, (q < PARTS // 2) == (way == 0))

    def ring_sum(low, high):
        @pl.loop(low, high)
        def _(step):
            share_copy(dest(0, step), False).wait_recv()
            share_copy(dest(1, step), False).wait_recv()
            for q in range(PARTS):
                for way in (0, 1):
                    sum_step(way, step, q, True)

    middle = max(2, half // 2)
    late = max(middle, half - 1)
    ring_sum(2, middle)

    total = q2[...]
    for j in range(1, far):
        far_copy(j, j).wait_recv()
        total = total + r3[j]
    q3[...] = total * scale

    def done_copy(j, source_col):
        return send(q3, r4.at[pl.ds(source_col * slab, slab)], e_send.at[j], e_recv.at[j], (row, peer(j)))

    @pl.loop(1, n_col)
    def _(j):
        slab_copy(j, col).wait_send()
        done_copy(j, col).start()

    r4[pl.ds(pl.multiple_of(col * slab, slab), slab), :] = q3[...]
    ring_sum(middle, late)

    @pl.loop(1, n_col)
    def _(j):
        done_copy(j, lax.rem(col + n_col - j, n_col)).wait_recv()

    join = send(r4, full, d_send.at[1], d_recv.at[1], mate_id)
    join.start()
    ring_sum(late, half)

    share_copy(z, False).wait_recv()
    for q in range(PARTS):
        rows = rows_of(q)
        total = mine(z, q)
        for way in (0, 1):
            sum_copy(way, half - 1, q).wait_recv()
            total = total + landed[way, half - 1, rows, :].astype(F32)
        gf_ref[rows, :] = total.astype(BF16)

    join.wait_recv()
    split.wait_send()
    own_rows = pl.ds(pl.multiple_of(core * share, share), share)
    other_rows = pl.ds(pl.multiple_of(other * share, share), share)
    gw_ref[own_rows, :] = r4[:, 0:width]
    gw_ref[other_rows, :] = full[:, 0:width]
    wide[own_rows, 0:tb] = r4[:, width:]
    wide[other_rows, 0:tb] = full[:, width:]
    gb_ref[...] = wide[:, 0:tb].T[0:1, :]

    @pl.loop(0, half - 1)
    def _(step):
        for q in range(PARTS):
            for way in (0, 1):
                ring_copy(way, step, q).wait_send()

    for q in range(PARTS):
        ring_copy(0 if q < PARTS // 2 else 1, half - 1, q).wait_send()

    @pl.loop(0, nz)
    def _(zz):
        for q in range(PARTS):
            mate_copy(zz, q).wait_send()
        share_copy(zz, True).wait_send()

    @pl.loop(1, n_col)
    def _(j):
        plane_copy(j).wait_send()
        grad_copy(j, col).wait_send()
        done_copy(j, col).wait_send()

    join.wait_send()
    for j in range(1, group):
        near_copy(j, j).wait_send()
    for j in range(1, far):
        far_copy(j, j).wait_send()
    for q in range(PARTS):
        sum_copy(0 if q < PARTS // 2 else 1, 0, q).wait_send()

    @pl.loop(1, half)
    def _(step):
        for q in range(PARTS):
            for way in (0, 1):
                sum_copy(way, step, q).wait_send()


def on_device(
    features, tiles, tile_rows, tile_cols, tile_count, weight, bias, cotangent, label_mask
):
    n_row = lax.axis_size("row")
    n_col = lax.axis_size("col")
    nz = n_row // 2
    half = nz // 2
    group = 4 if nz >= 16 else 2
    far = nz // group
    tb = tiles.shape[-1]
    slots = tiles.shape[2]
    width = features.shape[2]
    share = width // 2
    slab = share // n_col
    lanes = width + tb
    scale = 1.0 / math.sqrt(n_row * n_col * tb)
    dims = (nz, n_col, slots, tb, width, group, scale)
    vmem = pl.BlockSpec(memory_space=pltpu.VMEM)
    smem = pl.BlockSpec(memory_space=pltpu.SMEM)
    dma = pltpu.SemaphoreType.DMA
    hidden, gw, gb, gf = pl.pallas_call(
        functools.partial(kernel, dims),
        out_shape=(
            jax.ShapeDtypeStruct((tb, width), BF16),
            jax.ShapeDtypeStruct((width, width), F32),
            jax.ShapeDtypeStruct((1, width), F32),
            jax.ShapeDtypeStruct((tb, width), BF16),
        ),
        in_specs=[vmem, pl.BlockSpec(memory_space=pl.ANY), smem, smem, smem] + [vmem] * 6,
        out_specs=(vmem,) * 4,
        scratch_shapes=[
            pltpu.VMEM((slots, tb, tb), BF16),
            pltpu.VMEM((slots, tb, tb), BF16),
            pltpu.VMEM((n_row, tb, width), BF16),
            pltpu.VMEM((slots, tb, width), F32),
            pltpu.VMEM((n_col, tb, width), BF16),
            pltpu.VMEM((n_col, tb, width), BF16),
            pltpu.VMEM((n_col, tb, width), BF16),
            pltpu.VMEM((n_row, tb, width), BF16),
            pltpu.VMEM((nz, tb, width), BF16),
            pltpu.VMEM((2, half, tb, width), BF16),
            pltpu.VMEM((2, half, tb, width), BF16),
            pltpu.VMEM((8, tb), jnp.int32),
            pltpu.SMEM((8, tb), jnp.int32),
            pltpu.VMEM((width, lanes), F32),
            pltpu.VMEM((share, lanes), F32),
            pltpu.VMEM((share, lanes), F32),
            pltpu.VMEM((n_col, slab, lanes), F32),
            pltpu.VMEM((slab, lanes), F32),
            pltpu.VMEM((group, slab, lanes), F32),
            pltpu.VMEM((slab, lanes), F32),
            pltpu.VMEM((far, slab, lanes), F32),
            pltpu.VMEM((slab, lanes), F32),
            pltpu.VMEM((share, lanes), F32),
            pltpu.VMEM((share, lanes), F32),
            dma, dma,
            dma((2, half, PARTS)), dma((2, half, PARTS)),
            dma((nz, PARTS)), dma((nz, PARTS)),
            dma((n_col,)), dma((n_col,)),
            dma((n_col,)), dma((n_col,)),
            dma((nz,)), dma((nz,)),
            dma((n_col,)), dma((n_col,)),
            dma((group + far,)), dma((group + far,)),
            dma((2,)), dma((2,)),
            dma((2, half, PARTS)), dma((2, half, PARTS)),
            dma((n_col,)), dma((n_col,)),
        ],
        compiler_params=pltpu.CompilerParams(
            collective_id=0, has_side_effects=True, vmem_limit_bytes=56 << 20
        ),
        name="graph_layer",
    )(
        features[0], tiles[0, 0], tile_rows[0], tile_cols[0], tile_count,
        tile_rows[0], tile_cols[0], weight, bias[None], cotangent[0], label_mask,
    )
    return hidden[None], gw, gb[0], gf[None]


def solution(mesh):
    return jax.shard_map(
        on_device,
        mesh=mesh,
        in_specs=(
            P("col", "row", None),
            P("row", "col", None, None, None),
            P("row", "col", None),
            P("row", "col", None),
            P("row", "col"),
            P(),
            P(),
            P("row", "col", None),
            P("row", "col"),
        ),
        out_specs=(P("row", "col", None), P(), P(), P("col", "row", None)),
        check_vma=False,
    )
```

time: 870 us -> 140 us (0.16)
  the two profiles are of different devices: /device:TPU:1 before, /device:TPU:32 now
where the time goes in v1:
time: 140 us; the launch traced here: 139 us
  Pallas kernels  132 us (94%)
  local copies, waits for them, and re-layouts  5.81 us (4%)
    pallas_call x1, Pallas kernels, on_device(): pl.pallas_call(functools.partial(kernel, dims), out_shape=(jax.ShapeDtype...  132 us
    unnamed x4, local copies, waits for them, and re-layouts  5.81 us

profile of v1, /device:TPU:32, one launch (start us, length us, event | category | flops | bytes accessed | tf_op | source)
XLA Modules:
  0.0 139.5 jit_solution(3805983042555510686)
XLA Ops:
  1.3 132.4 %graph_layer.1 = (bf16[128,256]{1,0:T(8,128)(2,1)}, f32[256,256]{1,0:T(8,128)}, f32[1,256]{1,0:T(1,128)}, bf16[128,256]{1,0:T(8,128)(2,1)}) custom-call(bf16[128,256]{1,0:T(8,128)(2,1)} %bitcast.10, bf16[56,128,128]{2,1,0:T(8,128)(2,1)} %bitcast.9, s32[1,56]{1,0:T(1,128)} %bitcast.14, s32[1,56]{1,0:T(1,128)} %bitcast.16, s32[1,1]{1,0:T(1,128)S(6)} %copy.17.count_s, ...), custom_call_target="tpu_custom_call" | custom-call | tf_op jit(solution)/shard_map/graph_layer/pallas_call | solution.py:446
  133.7 1.5 %copy.18 = bf16[1,128,256]{2,1,0:T(8,128)(2,1)} copy(bf16[1,128,256]{2,1,0:T(8,128)(2,1)} %bitcast.13) | data formatting | bytes 131072
  135.1 1.7 %copy.19 = f32[256,256]{1,0:T(8,128)} copy(f32[256,256]{1,0:T(8,128)} %get-tuple-element.17) | data formatting | bytes 524288
  136.8 1.2 copy.20
  138.0 1.5 %copy.21 = bf16[1,128,256]{2,1,0:T(8,128)(2,1)} copy(bf16[1,128,256]{2,1,0:T(8,128)(2,1)} %bitcast.12) | data formatting | bytes 131072

commit v2 on v1

--- a/solution.py
+++ b/solution.py
@@ -10,6 +10,7 @@
 
 MESH = pl.DeviceIdType.MESH
 PARTS = 4
+UNROLL = 8
 F32 = jnp.float32
 BF16 = jnp.bfloat16
 
@@ -89,11 +90,7 @@
     def _(j):
         greet((row, peer(j)))
 
-    for j in range(1, group):
-        greet(at_z(near_z(j)))
-    for j in range(1, far):
-        greet(at_z(far_z(j)))
-    pl.semaphore_wait(barrier, 3 + (n_col - 1) + (group - 1) + (far - 1))
+    pl.semaphore_wait(barrier, 3 + (n_col - 1))
 
     def send(src, dst, send_sem, recv_sem, who):
         return pltpu.make_async_remote_copy(
@@ -178,14 +175,16 @@
             send(block, block, c_send.at[zz, q], c_recv.at[zz, q], mate_id).wait_recv()
 
     def products(blocks, line, index_s, values):
-        def one(k, total):
-            slot = table_s[line, k]
-            product = jnp.dot(blocks[slot], values[index_s[0, slot]], preferred_element_type=F32)
-            total = jnp.where(table_s[line + 1, k] == 1, product, total + product)
-            prod[k] = total
+        def some(turn, total):
+            for i in range(UNROLL):
+                k = turn * UNROLL + i
+                slot = table_s[line, k]
+                product = jnp.dot(blocks[slot], values[index_s[0, slot]], preferred_element_type=F32)
+                total = jnp.where(table_s[line + 1, k] == 1, product, total + product)
+                prod[k] = total
             return total
 
-        lax.fori_loop(0, slots, one, jnp.zeros((tb, width), F32))
+        lax.fori_loop(0, slots // UNROLL, some, jnp.zeros((tb, width), F32))
 
     def run_total(line, i):
         kept = table_s[line + 3, i] > 0
@@ -253,6 +252,17 @@
     def _(j):
         grad_copy(j, lax.rem(col + n_col - j, n_col)).wait_recv()
 
+    products(tiles_t, 4, rows_s, grads)
+
+    def share_copy(zz, send_to_mate):
+        src = back.at[2 * zz + (other if send_to_mate else core)]
+        return send(src, mate.at[zz], m_send.at[zz], m_recv.at[zz], mate_id)
+
+    def fill(zz):
+        for which in (core, other):
+            back[2 * zz + which] = run_total(4, 2 * zz + which).astype(BF16)
+        share_copy(zz, True).start()
+
     def add_slab(j, total):
         back_col = lax.rem(col + n_col - j, n_col)
         slab_copy(j, back_col).wait_recv()
@@ -269,34 +279,6 @@
 
     for j in range(1, group):
         near_copy(j, j).start()
-
-    products(tiles_t, 4, rows_s, grads)
-
-    def share_copy(zz, send_to_mate):
-        src = back.at[2 * zz + (other if send_to_mate else core)]
-        return send(src, mate.at[zz], m_send.at[zz], m_recv.at[zz], mate_id)
-
-    def fill(zz):
-        for which in (core, other):
-            back[2 * zz + which] = run_total(4, 2 * zz + which).astype(BF16)
-        share_copy(zz, True).start()
-
-    fill(lax.rem(z + half, nz))
-
-    @pl.loop(1, half)
-    def _(step):
-        fill(lax.rem(z + half - step, nz))
-        fill(lax.rem(z + half + step, nz))
-
-    fill(z)
-
-    total = q1[...]
-    for j in range(1, group):
-        near_copy(j, j).wait_recv()
-        total = total + r2[j]
-    q2[...] = total
-    for j in range(1, far):
-        far_copy(j, j).start()
 
     def dest(way, step):
         return lax.rem(z + half - step, nz) if way == 0 else lax.rem(z + half + step, nz)
@@ -321,26 +303,51 @@
         stage[way, step, rows, :] = total.astype(BF16)
         sum_copy(way, step, q).start()
 
-    share_copy(dest(0, 0), False).wait_recv()
-    for q in range(PARTS):
-        sum_step(0 if q < PARTS // 2 else 1, 0, q, False)
-    share_copy(dest(0, 1), False).wait_recv()
-    share_copy(dest(1, 1), False).wait_recv()
-    for q in range(PARTS):
-        for way in (0, 1):
-            sum_step(way, 1, q, (q < PARTS // 2) == (way == 0))
-
     def ring_sum(low, high):
         @pl.loop(low, high)
         def _(step):
+            fill(dest(0, step + 2))
+            fill(dest(1, step + 2))
             share_copy(dest(0, step), False).wait_recv()
             share_copy(dest(1, step), False).wait_recv()
             for q in range(PARTS):
                 for way in (0, 1):
                     sum_step(way, step, q, True)
 
-    middle = max(2, half // 2)
-    late = max(middle, half - 1)
+    def ring_tail(step):
+        if step == half - 2:
+            fill(z)
+        share_copy(dest(0, step), False).wait_recv()
+        share_copy(dest(1, step), False).wait_recv()
+        for q in range(PARTS):
+            for way in (0, 1):
+                sum_step(way, step, q, True)
+
+    fill(dest(0, 0))
+    fill(dest(0, 1))
+    fill(dest(1, 1))
+    share_copy(dest(0, 0), False).wait_recv()
+    for q in range(PARTS):
+        sum_step(0 if q < PARTS // 2 else 1, 0, q, False)
+    fill(dest(0, 2))
+    fill(dest(1, 2))
+    fill(dest(0, 3))
+    fill(dest(1, 3))
+    share_copy(dest(0, 1), False).wait_recv()
+    share_copy(dest(1, 1), False).wait_recv()
+    for q in range(PARTS):
+        for way in (0, 1):
+            sum_step(way, 1, q, (q < PARTS // 2) == (way == 0))
+
+    total = q1[...]
+    for j in range(1, group):
+        near_copy(j, j).wait_recv()
+        total = total + r2[j]
+    q2[...] = total
+    for j in range(1, far):
+        far_copy(j, j).start()
+
+    middle = max(2, half // 2 + 1)
     ring_sum(2, middle)
 
     total = q2[...]
@@ -358,7 +365,9 @@
         done_copy(j, col).start()
 
     r4[pl.ds(pl.multiple_of(col * slab, slab), slab), :] = q3[...]
-    ring_sum(middle, late)
+    ring_sum(middle, half - 2)
+    ring_tail(half - 2)
+    ring_tail(half - 1)
 
     @pl.loop(1, n_col)
     def _(j):
@@ -366,7 +375,6 @@
 
     join = send(r4, full, d_send.at[1], d_recv.at[1], mate_id)
     join.start()
-    ring_sum(late, half)
 
     share_copy(z, False).wait_recv()
     for q in range(PARTS):
@@ -421,6 +429,13 @@
         for q in range(PARTS):
             for way in (0, 1):
                 sum_copy(way, step, q).wait_send()
+
+
+def hand_over(hidden_in, gw_in, gb_in, gf_in, hidden_ref, gw_ref, gb_ref, gf_ref):
+    hidden_ref[...] = hidden_in[...]
+    gw_ref[...] = gw_in[...]
+    gb_ref[...] = gb_in[...]
+    gf_ref[...] = gf_in[...]
 
 
 def on_device(
@@ -491,13 +506,21 @@
             dma((n_col,)), dma((n_col,)),
         ],
         compiler_params=pltpu.CompilerParams(
-            collective_id=0, has_side_effects=True, vmem_limit_bytes=56 << 20
+            collective_id=0, has_side_effects=True, vmem_limit_bytes=63 << 20
         ),
         name="graph_layer",
     )(
         features[0], tiles[0, 0], tile_rows[0], tile_cols[0], tile_count,
         tile_rows[0], tile_cols[0], weight, bias[None], cotangent[0], label_mask,
     )
+    hidden, gw, gb, gf = pl.pallas_call(
+        hand_over,
+        out_shape=tuple(jax.ShapeDtypeStruct(x.shape, x.dtype) for x in (hidden, gw, gb, gf)),
+        in_specs=[vmem] * 4,
+        out_specs=(vmem,) * 4,
+        compiler_params=pltpu.CompilerParams(vmem_limit_bytes=63 << 20),
+        name="hand_over",
+    )(hidden, gw, gb, gf)
     return hidden[None], gw, gb[0], gf[None]
 
 

time: 140 us -> 117 us (0.84)
  the two profiles are of different devices: /device:TPU:32 before, /device:TPU:1 now
where the time goes in v2:
time: 117 us; the launch traced here: 116 us
  Pallas kernels  115 us (98%)
  between operations  1.29 us (1%)
    pallas_call x1, Pallas kernels, on_device(): pl.pallas_call(functools.partial(kernel, dims), out_shape=(jax.ShapeDtype...  113 us

profile of v2, /device:TPU:1, one launch (start us, length us, event | category | flops | bytes accessed | tf_op | source)
XLA Modules:
  0.0 116.2 jit_solution(14352147828532010798)
XLA Ops:
  1.3 113.2 %graph_layer.1 = (bf16[128,256]{1,0:T(8,128)(2,1)}, f32[256,256]{1,0:T(8,128)}, f32[1,256]{1,0:T(1,128)}, bf16[128,256]{1,0:T(8,128)(2,1)}) custom-call(bf16[128,256]{1,0:T(8,128)(2,1)} %bitcast.10, bf16[56,128,128]{2,1,0:T(8,128)(2,1)} %bitcast.9, s32[1,56]{1,0:T(1,128)} %bitcast.12, s32[1,56]{1,0:T(1,128)} %bitcast.14, s32[1,1]{1,0:T(1,128)S(6)} %copy.13.count_s, ...), custom_call_target="tpu_custom_call" | custom-call | tf_op jit(solution)/shard_map/graph_layer/pallas_call | solution.py:461
  114.5 1.7 %hand_over.1 = (bf16[128,256]{1,0:T(8,128)(2,1)}, f32[256,256]{1,0:T(8,128)}, f32[1,256]{1,0:T(1,128)}, bf16[128,256]{1,0:T(8,128)(2,1)}) custom-call(bf16[128,256]{1,0:T(8,128)(2,1)} %get-tuple-element.12.hidden_in, f32[256,256]{1,0:T(8,128)} %get-tuple-element.13.gw_in, f32[1,256]{1,0:T(1,128)} %get-tuple-element.14.gb_in, ...), custom_call_target="tpu_custom_call" | custom-call | tf_op jit(solution)/shard_map/hand_over/pallas_call | solution.py:516
